TPU v7x, 32 devices: a whole 2x2x4 slice. The times are simulated.
32 devices in a mesh: dev: 8 (over z, y), rep: 4 (over x, core).
Axes of the slice: x: 2, y: 2, z: 4, core: 2. Of those that a mesh axis runs over, the one named last changes fastest.
Arguments:
- spins: int32 [8, 64], P('dev'), may hold values 0 or 1
- activations: float32 [4, 8, 64, 128], P('rep', 'dev'), may hold values from 0 to 0.5
- gradients: float32 [4, 8, 64, 256], P('rep', 'dev'), may hold values from -0.1 to 0.3
Outputs:
- gram: float32 [8, 8], P('dev', 'rep')
Inputs may be any that keep to these rules, and one draw needn't show every extreme that they name: `spins`: 1 marks an occupied site, 0 an empty one.
All inputs are finite; a program needn't handle non-finite values. No bound on the sum of `spins` on one device may be relied on, other than what follows from the above.
Results may differ from a plain program's by a relative error of at most 0.0001.
Values sent between devices are 32-bit elements; how exact they have to be, the bound alone decides.
No kernel may reach another device: no remote copies, remote signals or barrier semaphores. Data moves between devices by JAX's collectives and lax.ppermute only.
A program may use at most 128 MiB of HBM per device.

v0:
```python
import jax
import jax.numpy as jnp
from jax import lax
from jax.sharding import PartitionSpec as P


def form_scores(act, grad, occupied):
    weighted = act * occupied[None, :, :, None]
    score = jnp.einsum("psra,psrb->spab", weighted, grad, precision=lax.Precision.HIGHEST)
    return score.reshape(score.shape[0], score.shape[1], -1)


def body(spins, activations, gradients):
    occupied = spins.astype(jnp.float32)
    all_act, all_grad = (
        lax.all_gather(activations, "rep", axis=0, tiled=True),
        lax.all_gather(gradients, "rep", axis=0, tiled=True),
    )
    score = form_scores(all_act, all_grad, occupied)
    moved = lax.all_to_all(score, "dev", split_axis=2, concat_axis=0, tiled=True)
    total = moved.shape[0]
    centered = moved - jnp.mean(moved, axis=0, keepdims=True)
    width = total // lax.axis_size("rep")
    begin = lax.axis_index("rep") * width
    columns = lax.dynamic_slice_in_dim(centered, begin, width, 0)
    partial_gram = jnp.einsum("spa,tpa->st", centered, columns, precision=lax.Precision.HIGHEST)
    return lax.psum_scatter(partial_gram / total, "dev", scatter_dimension=0, tiled=True)


def solution(mesh):
    return jax.shard_map(
        body,
        mesh=mesh,
        in_specs=(P("dev", None), P("rep", "dev", None, None), P("rep", "dev", None, None)),
        out_specs=P("dev", "rep"),
        check_vma=False,
    )
```

profile of v0, /device:TPU:0, one launch (start us, length us, event | category | flops | bytes accessed | tf_op | source)
XLA Modules:
  0.0 278.7 jit_solution(6322244386527385481)
XLA Ops:
  0.0 7.4 %all_gather.7 = f32[4,1,64,256]{3,2,1,0:T(8,128)S(1)} all-gather(f32[1,1,64,256]{3,2,1,0:T(8,128)} %param.5), channel_id=1, replica_groups=mesh['dev'=8,'rep'=4] {'rep'}, dimensions={0}, use_global_device_ids=true | all-gather | bytes 327680 | tf_op jit(solution)/shard_map/all_gather | solution.py:17
  7.4 5.6 %all_gather.6 = f32[4,1,64,128]{3,2,1,0:T(8,128)S(1)} all-gather(f32[1,1,64,128]{3,2,1,0:T(8,128)} %param.4), channel_id=1, replica_groups=mesh['dev'=8,'rep'=4] {'rep'}, dimensions={0}, use_global_device_ids=true | all-gather | bytes 163840 | tf_op jit(solution)/shard_map/all_gather | solution.py:16
  13.0 0.7 convert_bitcast_fusion
  13.7 0.7 fusion.1
  14.4 8.7 %copy.7 = f32[4,128,256]{0,2,1:T(8,128)} copy(f32[4,128,256]{2,1,0:T(8,128)S(1)} %fusion.1) | data formatting | bytes 1048576 | tf_op jit(solution)/shard_map/reshape | solution.py:10
  23.1 0.5 broadcast.13
  23.6 146.5 %reduce.1 = f32[32768,4]{1,0:T(8,128)} reduce(f32[32768,1,4]{2,1,0:T(1,128)} %bitcast.23, f32[]{:T(128)} %broadcast.13), dimensions={1}, to_apply=%bitcast.20.reduce_sub_computation | reduce | bytes 1048580
  170.1 16.0 %reshape.23 = f32[8,1,16384]{2,1,0:T(1,128)} reshape(f32[32768,4]{1,0:T(8,128)} %reduce.1) | data formatting | bytes 1048576
  186.1 5.9 %all-to-all-start = ((f32[8,1,16384]{2,1,0:T(1,128)}), f32[8,1,16384]{2,1,0:T(1,128)S(1)}, u32[]{:S(2)}, u32[]{:S(2)}) async-start(f32[8,1,16384]{2,1,0:T(1,128)} %reshape.23), calls=%async_computation | async-start | bytes 1048576 | tf_op jit(solution)/shard_map/all_to_all | solution.py:20
  191.9 15.0 %all-to-all-done = f32[8,1,16384]{2,1,0:T(1,128)S(1)} async-done(((f32[8,1,16384]{2,1,0:T(1,128)}), f32[8,1,16384]{2,1,0:T(1,128)S(1)}, u32[]{:S(2)}, u32[]{:S(2)}) %all-to-all-start) | async-done | bytes 524320 | tf_op jit(solution)/shard_map/all_to_all | solution.py:20
  206.9 1.9 reduce.2
  208.8 0.0 copy-start
  208.8 37.3 %reshape.24 = f32[32768,1,4]{2,1,0:T(1,128)} reshape(f32[8,16384]{1,0:T(8,128)S(1)} %reduce.2) | data formatting | bytes 1048576
  246.1 9.8 %copy.8 = f32[1,4,8,4096]{3,2,1,0:T(8,128)S(1)} copy(f32[1,4,8,4096]{1,3,2,0:T(8,128)} %bitcast.24) | data formatting | bytes 1048576 | tf_op jit(solution)/shard_map/all_to_all | solution.py:20
  255.9 0.1 bitcast_reduce_fusion
  256.1 0.1 bitcast_subtract_fusion
  256.1 1.2 fusion
  257.3 0.0 copy-done
  257.3 0.7 dynamic-slice
  258.0 19.5 %all-reduce = f32[8,2]{1,0:T(8,128)S(1)} all-reduce(f32[8,2]{1,0:T(8,128)S(1)} %fusion), channel_id=2, replica_groups=mesh['dev'=8,'rep'=4] {'dev'}, use_global_device_ids=true, to_apply=%region_1.0.clone | all-reduce | flops 16 | bytes 128
  277.5 1.2 constant_dynamic-slice_fusion
  (1 shorter events, 0.0 us)
Async XLA Ops:
  186.1 20.9 %all-to-all-start = ((f32[8,1,16384]{2,1,0:T(1,128)}), f32[8,1,16384]{2,1,0:T(1,128)S(1)}, u32[]{:S(2)}, u32[]{:S(2)}) async-start(f32[8,1,16384]{2,1,0:T(1,128)} %reshape.23), calls=%async_computation | async-start | bytes 1048576 | tf_op jit(solution)/shard_map/all_to_all | solution.py:20
  208.8 48.5 %copy-start = (u32[32]{0:T(128)S(1)}, u32[32]{0:T(128)}, u32[]{:S(2)}) copy-start(u32[32]{0:T(128)} %constant.22) | copy-start | bytes 388
where the time goes:
time: 279 us
  other arithmetic  149 us (53%)
  local copies, waits for them, and re-layouts  74.1 us (27%)
  blocking collectives  32.5 us (12%)
  waiting for transfers between devices  15 us (5%)
  starting transfers between devices  5.88 us (2%)
    unnamed x1, other arithmetic  147 us
    unnamed x7, local copies, waits for them, and re-layouts  55.7 us
    unnamed x1, blocking collectives  19.5 us
    all_to_all x1, waiting for transfers between devices, body(): lax.all_to_all(score, 'dev', split_axis=2, concat_axis=0, tiled=True)  15 us
    all_to_all x1, local copies, waits for them, and re-layouts, body(): lax.all_to_all(score, 'dev', split_axis=2, concat_axis=0, tiled=True)  9.77 us
    reshape x1, local copies, waits for them, and re-layouts, form_scores(): return score.reshape(score.shape[0], score.shape[1], -1)  8.65 us
    all_gather x1, blocking collectives, body(): lax.all_gather(gradients, 'rep', axis=0, tiled=True)  7.42 us
    all_to_all x1, starting transfers between devices, body(): lax.all_to_all(score, 'dev', split_axis=2, concat_axis=0, tiled=True)  5.88 us
  transfers between devices with their start and end apart: 1, of which 1 were waited for; matrix products, arithmetic and copies ran while one was open for 0% of the time, Pallas kernels for 0%

commit v1 on v0

v1 whole, which is shorter than its diff:
```python
import functools

import jax
import jax.numpy as jnp
from jax import lax
from jax.experimental import pallas as pl
from jax.experimental.pallas import tpu as pltpu
from jax.sharding import PartitionSpec as P

LANES = 128


def score_kernel(pieces, spins_ref, act_ref, grad_ref, score_ref):
    occupied = spins_ref[...].astype(jnp.float32)
    weighted = act_ref[...].T * occupied
    score = jnp.dot(
        weighted,
        grad_ref[...],
        precision=lax.Precision.HIGHEST,
        preferred_element_type=jnp.float32,
    )
    rows = score.shape[0] // pieces
    parts = score.shape[1] // LANES
    for piece in range(pieces):
        for part in range(parts):
            score_ref[pl.ds((piece * parts + part) * rows, rows), :] = score[
                piece * rows : (piece + 1) * rows, part * LANES : (part + 1) * LANES
            ]


def gram_kernel(samples, copies, moved_ref, gram_ref):
    rows = moved_ref.shape[0] // samples
    gram = jnp.zeros((samples, samples), jnp.float32)
    for row in range(rows):
        score = moved_ref[pl.ds(row, samples, stride=rows), :]
        centered = score - jnp.sum(score, axis=0, keepdims=True) * (1.0 / samples)
        gram = gram + lax.dot_general(
            centered,
            centered,
            (((1,), (1,)), ((), ())),
            precision=lax.Precision.HIGHEST,
            preferred_element_type=jnp.float32,
        )
    gram = gram / samples
    for s in range(samples):
        gram_ref[pl.ds(s * copies, copies), pl.ds(0, samples)] = jnp.broadcast_to(gram[s : s + 1, :], (copies, samples))


def vmem(count):
    return [pl.BlockSpec(memory_space=pltpu.VMEM)] * count


def body(spins, activations, gradients):
    n_dev, n_rep = lax.axis_size("dev"), lax.axis_size("rep")
    act, grad = activations[0, 0], gradients[0, 0]
    channels, outputs = act.shape[1], grad.shape[1]
    score = pl.pallas_call(
        functools.partial(score_kernel, n_dev),
        out_shape=jax.ShapeDtypeStruct((channels * outputs // LANES, LANES), jnp.float32),
        in_specs=vmem(3),
        out_specs=vmem(1)[0],
        name="score",
    )(spins, act, grad)
    moved = lax.all_to_all(score, "dev", split_axis=0, concat_axis=0, tiled=True)
    partial = pl.pallas_call(
        functools.partial(gram_kernel, n_dev, n_rep),
        out_shape=jax.ShapeDtypeStruct((n_dev * n_rep, LANES), jnp.float32),
        in_specs=vmem(1),
        out_specs=vmem(1)[0],
        name="gram",
    )(moved)
    parts = lax.all_to_all(partial, ("dev", "rep"), split_axis=0, concat_axis=0, tiled=True)
    total = jnp.sum(parts, axis=0, keepdims=True)
    width = n_dev // n_rep
    return lax.dynamic_slice_in_dim(total, lax.axis_index("rep") * width, width, 1)


def solution(mesh):
    return jax.shard_map(
        body,
        mesh=mesh,
        in_specs=(P("dev", None), P("rep", "dev", None, None), P("rep", "dev", None, None)),
        out_specs=P("dev", "rep"),
        check_vma=False,
    )
```

time: 279 us -> 29.3 us (0.11)
  other arithmetic: 149 us -> 0.05 us
  local copies, waits for them, and re-layouts: 74.1 us -> 0.59 us
  blocking collectives: 32.5 us -> 14.8 us
  waiting for transfers between devices: 15 us -> 7.17 us
  Pallas kernels: 0 us -> 3.97 us
  starting transfers between devices: 5.88 us -> 2.48 us
    unnamed x1 -> x0, other arithmetic: 147 us -> none
    unnamed x7 -> x0, local copies, waits for them, and re-layouts: 55.7 us -> none
    unnamed x1 -> x0, blocking collectives: 19.5 us -> none
    all_to_all x0 -> x1, blocking collectives: none -> 14.8 us  [body(): lax.all_to_all(score, 'dev', split_axis=0, concat_axis=0, tiled=True)]
    all_gather x2 -> x0, blocking collectives: 13 us -> none  [the longest x1 7.42 us: body(): lax.all_gather(gradients, 'rep', axis=0, tiled=True)]
    all_to_all x1 -> x0, local copies, waits for them, and re-layouts: 9.77 us -> none  [body(): lax.all_to_all(score, 'dev', split_axis=2, concat_axis=0, tiled=True)]
    reshape x1 -> x0, local copies, waits for them, and re-layouts: 8.65 us -> none  [form_scores(): return score.reshape(score.shape[0], score.shape[1], -1)]
    all_to_all x1, waiting for transfers between devices: 15 us -> 7.17 us  [body(): lax.all_to_all(partial, ('dev', 'rep'), split_axis=0, concat_axis=0, tile...]
where the time goes in v1:
time: 29.3 us; the launch traced here: 29 us
  blocking collectives  14.8 us (51%)
  waiting for transfers between devices  7.17 us (24%)
  Pallas kernels  3.97 us (14%)
  starting transfers between devices  2.48 us (8%)
  local copies, waits for them, and re-layouts  0.59 us (2%)
    all_to_all x1, blocking collectives, body(): lax.all_to_all(score, 'dev', split_axis=0, concat_axis=0, tiled=True)  14.8 us
    all_to_all x1, waiting for transfers between devices, body(): lax.all_to_all(partial, ('dev', 'rep'), split_axis=0, concat_axis=0, tile...  7.17 us
    all_to_all x1, starting transfers between devices, body(): lax.all_to_all(partial, ('dev', 'rep'), split_axis=0, concat_axis=0, tile...  2.48 us
    pallas_call x1, Pallas kernels, body(): pl.pallas_call(functools.partial(gram_kernel, n_dev, n_rep), out_shape=ja...  2.12 us
    pallas_call x1, Pallas kernels, body(): pl.pallas_call(functools.partial(score_kernel, n_dev), out_shape=jax.Shap...  1.84 us
  transfers between devices with their start and end apart: 1, of which 1 were waited for; matrix products, arithmetic and copies ran while one was open for 0% of the time, Pallas kernels for 0%

profile of v1, /device:TPU:0, one launch (start us, length us, event | category | flops | bytes accessed | tf_op | source)
XLA Modules:
  0.0 29.0 jit_solution(6883262415032529466)
XLA Ops:
  0.0 1.8 %score.1 = f32[256,128]{1,0:T(8,128)} custom-call(s32[1,64]{1,0:T(1,128)} %spins_ref.1, f32[64,128]{1,0:T(8,128)} %bitcast.13, f32[64,256]{1,0:T(8,128)} %bitcast.11), custom_call_target="tpu_custom_call" | custom-call | tf_op jit(solution)/shard_map/score/pallas_call | solution.py:57
  1.8 14.8 %all_to_all.20 = f32[8,32,128]{2,1,0:T(8,128)} all-to-all(f32[8,32,128]{2,1,0:T(8,128)} %bitcast.9), channel_id=1, replica_groups=mesh['dev'=8,'rep'=4] {'dev'}, dimensions={0} | all-to-all | bytes 262144 | tf_op jit(solution)/shard_map/all_to_all | solution.py:64
  16.6 2.1 %gram.1 = f32[32,128]{1,0:T(8,128)} custom-call(f32[256,128]{1,0:T(8,128)} %bitcast.10), custom_call_target="tpu_custom_call" | custom-call | tf_op jit(solution)/shard_map/gram/pallas_call | solution.py:65
  18.7 2.5 %all-to-all-start.1 = ((f32[32,1,128]{2,1,0:T(1,128)}), f32[32,1,128]{2,1,0:T(1,128)S(1)}, u32[]{:S(2)}, u32[]{:S(2)}) async-start(f32[32,1,128]{2,1,0:T(1,128)} %bitcast.12), calls=%async_computation.1 | async-start | bytes 32768 | tf_op jit(solution)/shard_map/all_to_all | solution.py:72
  21.2 7.2 %all-to-all-done.1 = f32[32,1,128]{2,1,0:T(1,128)S(1)} async-done(((f32[32,1,128]{2,1,0:T(1,128)}), f32[32,1,128]{2,1,0:T(1,128)S(1)}, u32[]{:S(2)}, u32[]{:S(2)}) %all-to-all-start.1) | async-done | bytes 16416 | tf_op jit(solution)/shard_map/all_to_all | solution.py:72
  28.4 0.1 reduce_sum.9
  28.4 0.6 %dynamic-slice_bitcast_fusion = f32[1,2]{1,0:T(1,128)} fusion(f32[128]{0:T(128)S(1)} %reduce_sum.9, s32[]{:T(128)S(6)} %select_n.3), kind=kLoop, calls=%fused_computation | loop fusion | bytes 20 | tf_op jit(solution)/shard_map/dynamic_slice | solution.py:75
Async XLA Ops:
  18.7 9.7 %all-to-all-start.1 = ((f32[32,1,128]{2,1,0:T(1,128)}), f32[32,1,128]{2,1,0:T(1,128)S(1)}, u32[]{:S(2)}, u32[]{:S(2)}) async-start(f32[32,1,128]{2,1,0:T(1,128)} %bitcast.12), calls=%async_computation.1 | async-start | bytes 32768 | tf_op jit(solution)/shard_map/all_to_all | solution.py:72

commit v2 on v1

--- a/solution.py
+++ b/solution.py
@@ -8,9 +8,19 @@
 from jax.sharding import PartitionSpec as P
 
 LANES = 128
+PARAMS = pltpu.CompilerParams(vmem_limit_bytes=4 * 1024 * 1024)
+VMEM = pl.BlockSpec(memory_space=pltpu.VMEM)
 
 
-def score_kernel(pieces, spins_ref, act_ref, grad_ref, score_ref):
+def score_kernel(pieces, spins_hbm, act_hbm, grad_hbm, score_ref, spins_ref, act_ref, grad_ref, sems):
+    copies = [
+        pltpu.make_async_copy(src, dst, sems.at[i])
+        for i, (src, dst) in enumerate(((grad_hbm, grad_ref), (act_hbm, act_ref), (spins_hbm, spins_ref)))
+    ]
+    for copy in copies:
+        copy.start()
+    for copy in copies:
+        copy.wait()
     occupied = spins_ref[...].astype(jnp.float32)
     weighted = act_ref[...].T * occupied
     score = jnp.dot(
@@ -28,7 +38,7 @@
             ]
 
 
-def gram_kernel(samples, copies, moved_ref, gram_ref):
+def gram_kernel(samples, shares, moved_ref, gram_ref, wide_ref):
     rows = moved_ref.shape[0] // samples
     gram = jnp.zeros((samples, samples), jnp.float32)
     for row in range(rows):
@@ -41,13 +51,12 @@
             precision=lax.Precision.HIGHEST,
             preferred_element_type=jnp.float32,
         )
-    gram = gram / samples
-    for s in range(samples):
-        gram_ref[pl.ds(s * copies, copies), pl.ds(0, samples)] = jnp.broadcast_to(gram[s : s + 1, :], (copies, samples))
-
-
-def vmem(count):
-    return [pl.BlockSpec(memory_space=pltpu.VMEM)] * count
+    wide_ref[...] = jnp.zeros_like(wide_ref)
+    wide_ref[:, pl.ds(0, samples)] = gram / samples
+    wide = wide_ref[...]
+    for share in range(shares):
+        turned = wide if share == 0 else pltpu.roll(wide, LANES - share * (samples // shares), axis=1)
+        gram_ref[pl.ds(share, samples, stride=shares), :] = turned
 
 
 def body(spins, activations, gradients):
@@ -57,22 +66,29 @@
     score = pl.pallas_call(
         functools.partial(score_kernel, n_dev),
         out_shape=jax.ShapeDtypeStruct((channels * outputs // LANES, LANES), jnp.float32),
-        in_specs=vmem(3),
-        out_specs=vmem(1)[0],
+        in_specs=[pl.BlockSpec(memory_space=pltpu.HBM)] * 3,
+        out_specs=VMEM,
+        scratch_shapes=[
+            pltpu.VMEM(spins.shape, spins.dtype),
+            pltpu.VMEM(act.shape, act.dtype),
+            pltpu.VMEM(grad.shape, grad.dtype),
+            pltpu.SemaphoreType.DMA((3,)),
+        ],
+        compiler_params=PARAMS,
         name="score",
-    )(spins, act, grad)
+    )(*(pltpu.with_memory_space_constraint(x, pltpu.HBM) for x in (spins, act, grad)))
     moved = lax.all_to_all(score, "dev", split_axis=0, concat_axis=0, tiled=True)
     partial = pl.pallas_call(
         functools.partial(gram_kernel, n_dev, n_rep),
         out_shape=jax.ShapeDtypeStruct((n_dev * n_rep, LANES), jnp.float32),
-        in_specs=vmem(1),
-        out_specs=vmem(1)[0],
+        in_specs=[VMEM],
+        out_specs=VMEM,
+        scratch_shapes=[pltpu.VMEM((n_dev, LANES), jnp.float32)],
+        compiler_params=PARAMS,
         name="gram",
     )(moved)
     parts = lax.all_to_all(partial, ("dev", "rep"), split_axis=0, concat_axis=0, tiled=True)
-    total = jnp.sum(parts, axis=0, keepdims=True)
-    width = n_dev // n_rep
-    return lax.dynamic_slice_in_dim(total, lax.axis_index("rep") * width, width, 1)
+    return jnp.sum(parts, axis=0, keepdims=True)[:, : n_dev // n_rep]
 
 
 def solution(mesh):

time: 29.3 us -> 26.5 us (0.904)
  blocking collectives: 14.8 us -> 23.8 us
  waiting for transfers between devices: 7.17 us -> 0 us
  starting transfers between devices: 2.48 us -> 0 us
  Pallas kernels: 3.97 us -> 1.94 us
  local copies, waits for them, and re-layouts: 0.59 us -> 0 us
  other arithmetic: 0.05 us -> 0.56 us
    all_to_all x0 -> x1, blocking collectives: none -> 9.37 us  [body(): lax.all_to_all(partial, ('dev', 'rep'), split_axis=0, concat_axis=0, tile...]
    all_to_all x1 -> x0, waiting for transfers between devices: 7.17 us -> none  [body(): lax.all_to_all(partial, ('dev', 'rep'), split_axis=0, concat_axis=0, tile...]
    all_to_all x1 -> x0, starting transfers between devices: 2.48 us -> none  [body(): lax.all_to_all(partial, ('dev', 'rep'), split_axis=0, concat_axis=0, tile...]
    pallas_call x1, Pallas kernels: 2.12 us -> 0.76 us  [body(): pl.pallas_call(functools.partial(gram_kernel, n_dev, n_rep), out_shape=ja...]
    pallas_call x1, Pallas kernels: 1.84 us -> 1.18 us  [body(): pl.pallas_call(functools.partial(score_kernel, n_dev), out_shape=jax.Shap...]
    dynamic_slice x1 -> x0, local copies, waits for them, and re-layouts: 0.59 us -> none  [body(): lax.dynamic_slice_in_dim(total, lax.axis_index('rep') * width, width, 1)]
    reduce_sum x1, other arithmetic: 0.05 us -> 0.56 us  [body(): return jnp.sum(parts, axis=0, keepdims=True)[:, :n_dev // n_rep]]
    all_to_all x1, blocking collectives: 14.8 us -> 14.5 us  [body(): lax.all_to_all(score, 'dev', split_axis=0, concat_axis=0, tiled=True)]
  transfers between devices with their start and end apart: 1 -> 0, of which waited for: 1 -> 0; matrix products, arithmetic and copies ran while one was open for 0% -> 0% of each run, Pallas kernels for 0% -> 0%
where the time goes in v2:
time: 26.5 us; the launch traced here: 26.3 us
  blocking collectives  23.8 us (90%)
  Pallas kernels  1.94 us (7%)
  other arithmetic  0.56 us (2%)
    all_to_all x1, blocking collectives, body(): lax.all_to_all(score, 'dev', split_axis=0, concat_axis=0, tiled=True)  14.5 us
    all_to_all x1, blocking collectives, body(): lax.all_to_all(partial, ('dev', 'rep'), split_axis=0, concat_axis=0, tile...  9.37 us
    pallas_call x1, Pallas kernels, body(): pl.pallas_call(functools.partial(score_kernel, n_dev), out_shape=jax.Shap...  1.18 us
    pallas_call x1, Pallas kernels, body(): pl.pallas_call(functools.partial(gram_kernel, n_dev, n_rep), out_shape=ja...  0.76 us
    reduce_sum x1, other arithmetic, body(): return jnp.sum(parts, axis=0, keepdims=True)[:, :n_dev // n_rep]  0.56 us

profile of v2, /device:TPU:0, one launch (start us, length us, event | category | flops | bytes accessed | tf_op | source)
XLA Modules:
  0.0 26.3 jit_solution(4052200531024937045)
XLA Ops:
  0.0 1.2 %score.1 = f32[256,128]{1,0:T(8,128)S(1)} custom-call(s32[1,64]{1,0:T(1,128)} %spins_hbm.1, f32[64,128]{1,0:T(8,128)} %bitcast.13, f32[64,256]{1,0:T(8,128)} %bitcast.12), custom_call_target="tpu_custom_call" | custom-call | tf_op jit(solution)/shard_map/score/pallas_call | solution.py:66
  1.2 14.5 %all_to_all.20 = f32[8,32,128]{2,1,0:T(8,128)S(1)} all-to-all(f32[8,32,128]{2,1,0:T(8,128)S(1)} %bitcast.9), channel_id=1, replica_groups=mesh['dev'=8,'rep'=4] {'dev'}, dimensions={0} | all-to-all | bytes 262144 | tf_op jit(solution)/shard_map/all_to_all | solution.py:80
  15.6 0.8 %gram.1 = f32[32,128]{1,0:T(8,128)S(1)} custom-call(f32[256,128]{1,0:T(8,128)S(1)} %bitcast.10), custom_call_target="tpu_custom_call" | custom-call | tf_op jit(solution)/shard_map/gram/pallas_call | solution.py:81
  16.4 9.4 %all_to_all.21 = f32[32,1,128]{2,1,0:T(1,128)S(1)} all-to-all(f32[32,1,128]{2,1,0:T(1,128)S(1)} %bitcast.11), channel_id=1, replica_groups=mesh['dev'=8,'rep'=4] {'dev','rep'}, dimensions={0} | all-to-all | bytes 32768 | tf_op jit(solution)/shard_map/all_to_all | solution.py:90
  25.8 0.6 %reduce_sum.9 = f32[128]{0:T(128)} reduce(f32[32,1,128]{2,1,0:T(1,128)S(1)} %all_to_all.21, f32[]{:T(128)} %constant.0.clone.1), dimensions={0,1}, to_apply=%region_0.0 | reduce | flops 3968 | bytes 16900 | tf_op jit(solution)/shard_map/reduce_sum | solution.py:91

commit v3 on v2

v3 whole, which is shorter than its diff:
```python
import functools

import jax
import jax.numpy as jnp
from jax import lax
from jax.experimental import pallas as pl
from jax.experimental.pallas import tpu as pltpu
from jax.sharding import PartitionSpec as P

LANES = 128
TERMS = 3
PARAMS = pltpu.CompilerParams(vmem_limit_bytes=4 * 1024 * 1024)
HBM = pl.BlockSpec(memory_space=pltpu.HBM)
VMEM = pl.BlockSpec(memory_space=pltpu.VMEM)
SMEM = pl.BlockSpec(memory_space=pltpu.SMEM)


def score_kernel(order, index_ref, spins_hbm, act_hbm, grad_hbm, index_out, score_ref, spins_ref, act_ref, grad_ref, sems):
    copies = [
        pltpu.make_async_copy(src, dst, sems.at[i])
        for i, (src, dst) in enumerate(((grad_hbm, grad_ref), (act_hbm, act_ref), (spins_hbm, spins_ref)))
    ]
    for copy in copies:
        copy.start()
    index_out[0] = index_ref[0]
    for copy in copies:
        copy.wait()
    occupied = spins_ref[...].astype(jnp.float32)
    weighted = act_ref[...].T * occupied
    score = jnp.dot(
        weighted,
        grad_ref[...],
        precision=lax.Precision.HIGHEST,
        preferred_element_type=jnp.float32,
    )
    slices = len(order) // 2
    rows = score.shape[0] // slices
    parts = score.shape[1] // LANES
    for place, owner in enumerate(order):
        piece = owner % slices
        for part in range(parts):
            score_ref[pl.ds((place * parts + part) * rows, rows), :] = score[
                piece * rows : (piece + 1) * rows, part * LANES : (part + 1) * LANES
            ]


def gram_kernel(order, goal, shares, index_ref, moved_ref, gram_ref, wide_ref):
    samples = len(order)
    rows = moved_ref.shape[0] // samples
    total = jnp.zeros((TERMS * samples, TERMS * samples), jnp.float32)
    for row in range(0, rows, 2):
        terms = []
        rest = []
        for step in range(2):
            score = moved_ref[pl.ds(row + step, samples, stride=rows), :]
            rest.append(score - jnp.sum(score, axis=0, keepdims=True) * (1.0 / samples))
        rest = jnp.concatenate(rest, axis=1)
        for _ in range(TERMS):
            term = rest.astype(jnp.bfloat16).astype(jnp.float32)
            terms.append(term)
            rest = rest - term
        stacked = jnp.concatenate(terms, axis=0).astype(jnp.bfloat16)
        total = total + lax.dot_general(
            stacked, stacked, (((1,), (1,)), ((), ())), preferred_element_type=jnp.float32
        )
    half = functools.reduce(jnp.add, [total[i * samples : (i + 1) * samples, :] for i in range(TERMS)])
    gram = functools.reduce(jnp.add, [half[:, i * samples : (i + 1) * samples] for i in range(TERMS)])
    wide_ref[...] = jnp.zeros_like(wide_ref)
    wide_ref[:, pl.ds(0, samples)] = gram / samples
    wide = wide_ref[...]
    width = samples // shares
    upper = index_ref[0] != 0
    members = len(goal)
    place = {owner: i for i, owner in enumerate(order)}
    for share in range(shares):
        column = place[share * width]
        turned = wide if column == 0 else pltpu.roll(wide, LANES - column, axis=1)
        for row in range(members // shares):
            low, high = place[row], place[row + members // shares]
            value = jnp.where(upper, turned[high : high + 1, :], turned[low : low + 1, :])
            gram_ref[pl.ds(goal.index(row * shares + share), 1), :] = value


def body(spins, activations, gradients):
    n_dev, n_rep = lax.axis_size("dev"), lax.axis_size("rep")
    act, grad = activations[0, 0], gradients[0, 0]
    channels, outputs = act.shape[1], grad.shape[1]
    width = n_dev // n_rep
    order = [place ^ (n_dev - width) for place in range(n_dev)]
    members = n_dev * n_rep // 2
    goal = [members - 1 - place for place in range(members)]
    size = channels * outputs // LANES // (n_dev // 2)
    index = (lax.axis_index("dev") // (n_dev // 2)).astype(jnp.int32).reshape(1)
    index, score = pl.pallas_call(
        functools.partial(score_kernel, order),
        out_shape=[
            jax.ShapeDtypeStruct((1,), jnp.int32),
            jax.ShapeDtypeStruct((n_dev * size, LANES), jnp.float32),
        ],
        in_specs=[SMEM, HBM, HBM, HBM],
        out_specs=[SMEM, VMEM],
        scratch_shapes=[
            pltpu.VMEM(spins.shape, spins.dtype),
            pltpu.VMEM(act.shape, act.dtype),
            pltpu.VMEM(grad.shape, grad.dtype),
            pltpu.SemaphoreType.DMA((3,)),
        ],
        compiler_params=PARAMS,
        name="score",
    )(index, *(pltpu.with_memory_space_constraint(x, pltpu.HBM) for x in (spins, act, grad)))
    moved = lax.all_to_all(score, "dev", split_axis=0, concat_axis=0, tiled=True, axis_index_groups=[order])
    partial = pl.pallas_call(
        functools.partial(gram_kernel, order, goal, n_rep),
        out_shape=jax.ShapeDtypeStruct((members, LANES), jnp.float32),
        in_specs=[SMEM, VMEM],
        out_specs=VMEM,
        scratch_shapes=[pltpu.VMEM((n_dev, LANES), jnp.float32)],
        compiler_params=PARAMS,
        name="gram",
    )(index, moved)
    groups = [[half * members + member for member in goal] for half in range(2)]
    parts = lax.all_to_all(
        partial, ("dev", "rep"), split_axis=0, concat_axis=0, tiled=True, axis_index_groups=groups
    )
    return jnp.sum(parts, axis=0, keepdims=True)[:, :width]


def solution(mesh):
    return jax.shard_map(
        body,
        mesh=mesh,
        in_specs=(P("dev", None), P("rep", "dev", None, None), P("rep", "dev", None, None)),
        out_specs=P("dev", "rep"),
        check_vma=False,
    )
```

time: 26.5 us -> 24.7 us (0.932)
  blocking collectives: 23.8 us -> 21.3 us
  Pallas kernels: 1.94 us -> 2.58 us
    all_to_all x1, blocking collectives: 9.37 us -> 7.28 us  [body(): lax.all_to_all(partial, ('dev', 'rep'), split_axis=0, concat_axis=0, tile...]
    pallas_call x2, Pallas kernels: 1.94 us -> 2.58 us  [the longest x1 1.39 us: body(): pl.pallas_call(functools.partial(score_kernel, order), out_shape=[jax.Sha...]
    all_to_all x1, blocking collectives: 14.5 us -> 14 us  [body(): lax.all_to_all(score, 'dev', split_axis=0, concat_axis=0, tiled=True, axi...]
where the time goes in v3:
time: 24.7 us; the launch traced here: 24.4 us
  blocking collectives  21.3 us (86%)
  Pallas kernels  2.58 us (10%)
  other arithmetic  0.54 us (2%)
    all_to_all x1, blocking collectives, body(): lax.all_to_all(score, 'dev', split_axis=0, concat_axis=0, tiled=True, axi...  14 us
    all_to_all x1, blocking collectives, body(): lax.all_to_all(partial, ('dev', 'rep'), split_axis=0, concat_axis=0, tile...  7.28 us
    pallas_call x1, Pallas kernels, body(): pl.pallas_call(functools.partial(score_kernel, order), out_shape=[jax.Sha...  1.39 us
    pallas_call x1, Pallas kernels, body(): pl.pallas_call(functools.partial(gram_kernel, order, goal, n_rep), out_sh...  1.2 us
    reduce_sum x1, other arithmetic, body(): return jnp.sum(parts, axis=0, keepdims=True)[:, :width]  0.54 us

profile of v3, /device:TPU:0, one launch (start us, length us, event | category | flops | bytes accessed | tf_op | source)
XLA Modules:
  0.0 24.4 jit_solution(9975596317027630460)
XLA Ops:
  0.0 1.4 %score.1 = (s32[1]{0:T(128)}, f32[512,128]{1,0:T(8,128)S(1)}) custom-call(s32[1]{0:T(128)} %bitcast.index_ref, s32[1,64]{1,0:T(1,128)} %spins_hbm.1, f32[64,128]{1,0:T(8,128)} %bitcast.14, f32[64,256]{1,0:T(8,128)} %bitcast.13), custom_call_target="tpu_custom_call" | custom-call | tf_op jit(solution)/shard_map/score/pallas_call | solution.py:94
  1.4 14.0 %all_to_all.20 = f32[8,64,128]{2,1,0:T(8,128)S(1)} all-to-all(f32[8,64,128]{2,1,0:T(8,128)S(1)} %bitcast.11), channel_id=1, replica_groups={{24,28,16,20,8,12,0,4},{25,29,17,21,9,13,1,5},{26,30,18,22,10,14,2,6},{..., dimensions={0} | all-to-all | bytes 524288 | tf_op jit(solution)/shard_map/all_to_all | solution.py:111
  15.4 1.2 %gram.1 = f32[16,128]{1,0:T(8,128)S(1)} custom-call(s32[1]{0:T(128)} %get-tuple-element.7.index_ref, f32[512,128]{1,0:T(8,128)S(1)} %bitcast.10), custom_call_target="tpu_custom_call" | custom-call | tf_op jit(solution)/shard_map/gram/pallas_call | solution.py:112
  16.6 7.3 %all_to_all.21 = f32[16,1,128]{2,1,0:T(1,128)S(1)} all-to-all(f32[16,1,128]{2,1,0:T(1,128)S(1)} %bitcast.12), channel_id=1, replica_groups={{15,14,13,12,11,10,9,8,7,6,5,4,3,2,1,0},{31,30,29,28,27,26,25,24,23,22,..., dimensions={0} | all-to-all | bytes 16384 | tf_op jit(solution)/shard_map/all_to_all | solution.py:122
  23.9 0.5 %reduce_sum.9 = f32[128]{0:T(128)} reduce(f32[16,1,128]{2,1,0:T(1,128)S(1)} %all_to_all.21, f32[]{:T(128)} %constant.23.clone.1), dimensions={0,1}, to_apply=%region_0.1 | reduce | flops 1920 | bytes 8708 | tf_op jit(solution)/shard_map/reduce_sum | solution.py:125

commit v4 on v3

v4 whole, which is shorter than its diff:
```python
import functools

import jax
import jax.numpy as jnp
from jax import lax
from jax.experimental import pallas as pl
from jax.experimental.pallas import tpu as pltpu
from jax.sharding import PartitionSpec as P

LANES = 128
UNROLLED = 16
PARAMS = pltpu.CompilerParams(vmem_limit_bytes=8 * 1024 * 1024)
HBM = pl.BlockSpec(memory_space=pltpu.HBM)
VMEM = pl.BlockSpec(memory_space=pltpu.VMEM)
SMEM = pl.BlockSpec(memory_space=pltpu.SMEM)


def score_kernel(order, index_ref, spins_hbm, act_hbm, grad_hbm, score_ref, spins_ref, act_ref, grad_ref, sems):
    copies = [
        pltpu.make_async_copy(src, dst, sems.at[i])
        for i, (src, dst) in enumerate(((grad_hbm, grad_ref), (act_hbm, act_ref), (spins_hbm, spins_ref)))
    ]
    for copy in copies:
        copy.start()
    for copy in copies:
        copy.wait()
    occupied = spins_ref[...].astype(jnp.float32)
    weighted = act_ref[...].T * occupied
    score = jnp.dot(
        weighted,
        grad_ref[...],
        precision=lax.Precision.HIGHEST,
        preferred_element_type=jnp.float32,
    )
    slices = len(order) // 2
    rows = score.shape[0] // slices
    parts = score.shape[1] // LANES
    for place, owner in enumerate(order):
        piece = owner % slices
        for part in range(parts):
            score_ref[pl.ds((place * parts + part) * rows, rows), :] = score[
                piece * rows : (piece + 1) * rows, part * LANES : (part + 1) * LANES
            ]


def each(count, step):
    if count <= UNROLLED:
        for i in range(count):
            step(i)
    else:
        pl.loop(0, count)(step)


def gram_kernel(order, members, shares, index_ref, moved_ref, gram_ref, centered_ref, lanes_ref):
    samples = len(order)
    width = samples // shares
    rows = moved_ref.shape[0] // samples
    scores = [moved_ref[pl.ds(place * rows, rows), :] for place in range(samples)]
    mean = functools.reduce(jnp.add, scores) * (1.0 / samples)
    for place, owner in enumerate(order):
        centered_ref[owner] = scores[place] - mean
    mine = members // shares
    first = index_ref[0] * mine

    def row_step(row):
        own = centered_ref[first + row]
        for share in range(shares):
            def column_step(column):
                product = own * centered_ref[share * width + column]
                place = members - 1 - (row * shares + share)
                lanes_ref[column, pl.ds(place, 1), :] = jnp.sum(product, axis=0, keepdims=True)

            each(width, column_step)

    each(mine, row_step)
    lane = lax.broadcasted_iota(jnp.int32, (members, LANES), 1)
    gram = jnp.zeros((members, LANES), jnp.float32)
    for column in range(width):
        gram = jnp.where(lane == column, jnp.sum(lanes_ref[column], axis=1, keepdims=True), gram)
    gram_ref[...] = gram * (1.0 / samples)


def body(spins, activations, gradients):
    n_dev, n_rep = lax.axis_size("dev"), lax.axis_size("rep")
    act, grad = activations[0, 0], gradients[0, 0]
    channels, outputs = act.shape[1], grad.shape[1]
    width = n_dev // n_rep
    order = [place ^ (n_dev - width) for place in range(n_dev)]
    members = n_dev * n_rep // 2
    goal = [members - 1 - place for place in range(members)]
    size = channels * outputs // LANES // (n_dev // 2)
    index = (lax.axis_index("dev") // (n_dev // 2)).astype(jnp.int32).reshape(1)
    score = pl.pallas_call(
        functools.partial(score_kernel, order),
        out_shape=jax.ShapeDtypeStruct((n_dev * size, LANES), jnp.float32),
        in_specs=[SMEM, HBM, HBM, HBM],
        out_specs=VMEM,
        scratch_shapes=[
            pltpu.VMEM(spins.shape, spins.dtype),
            pltpu.VMEM(act.shape, act.dtype),
            pltpu.VMEM(grad.shape, grad.dtype),
            pltpu.SemaphoreType.DMA((3,)),
        ],
        compiler_params=PARAMS,
        name="score",
    )(index, *(pltpu.with_memory_space_constraint(x, pltpu.HBM) for x in (spins, act, grad)))
    moved = lax.all_to_all(score, "dev", split_axis=0, concat_axis=0, tiled=True, axis_index_groups=[order])
    partial = pl.pallas_call(
        functools.partial(gram_kernel, order, members, n_rep),
        out_shape=jax.ShapeDtypeStruct((members, LANES), jnp.float32),
        in_specs=[SMEM, VMEM],
        out_specs=VMEM,
        scratch_shapes=[
            pltpu.VMEM((n_dev, size, LANES), jnp.float32),
            pltpu.VMEM((width, members, LANES), jnp.float32),
        ],
        compiler_params=PARAMS,
        name="gram",
    )(index, moved)
    groups = [[half * members + member for member in goal] for half in range(2)]
    parts = lax.all_to_all(
        partial, ("dev", "rep"), split_axis=0, concat_axis=0, tiled=True, axis_index_groups=groups
    )
    return jnp.sum(parts, axis=0, keepdims=True)[:, :width]


def solution(mesh):
    return jax.shard_map(
        body,
        mesh=mesh,
        in_specs=(P("dev", None), P("rep", "dev", None, None), P("rep", "dev", None, None)),
        out_specs=P("dev", "rep"),
        check_vma=False,
    )
```

time: 24.7 us -> 23.5 us (0.951)
  Pallas kernels: 2.58 us -> 1.41 us
    pallas_call x2, Pallas kernels: 2.58 us -> 1.41 us  [the longest x1 1.18 us: body(): pl.pallas_call(functools.partial(score_kernel, order), out_shape=jax.Shap...]
where the time goes in v4:
time: 23.5 us; the launch traced here: 23.2 us
  blocking collectives  21.3 us (91%)
  Pallas kernels  1.41 us (6%)
  other arithmetic  0.54 us (2%)
    all_to_all x1, blocking collectives, body(): lax.all_to_all(score, 'dev', split_axis=0, concat_axis=0, tiled=True, axi...  14 us
    all_to_all x1, blocking collectives, body(): lax.all_to_all(partial, ('dev', 'rep'), split_axis=0, concat_axis=0, tile...  7.27 us
    pallas_call x1, Pallas kernels, body(): pl.pallas_call(functools.partial(score_kernel, order), out_shape=jax.Shap...  1.18 us
    reduce_sum x1, other arithmetic, body(): return jnp.sum(parts, axis=0, keepdims=True)[:, :width]  0.54 us

profile of v4, /device:TPU:0, one launch (start us, length us, event | category | flops | bytes accessed | tf_op | source)
XLA Modules:
  0.0 23.2 jit_solution(13148806977121748615)
XLA Ops:
  0.0 1.2 %score.1 = f32[512,128]{1,0:T(8,128)S(1)} custom-call(s32[1]{0:T(128)} %bitcast.index_ref, s32[1,64]{1,0:T(1,128)} %spins_hbm.1, f32[64,128]{1,0:T(8,128)} %bitcast.14, f32[64,256]{1,0:T(8,128)} %bitcast.13), custom_call_target="tpu_custom_call" | custom-call | tf_op jit(solution)/shard_map/score/pallas_call | solution.py:93
  1.2 14.0 %all_to_all.20 = f32[8,64,128]{2,1,0:T(8,128)S(1)} all-to-all(f32[8,64,128]{2,1,0:T(8,128)S(1)} %bitcast.11), channel_id=1, replica_groups={{24,28,16,20,8,12,0,4},{25,29,17,21,9,13,1,5},{26,30,18,22,10,14,2,6},{..., dimensions={0} | all-to-all | bytes 524288 | tf_op jit(solution)/shard_map/all_to_all | solution.py:107
  15.2 0.2 gram.1
  15.4 7.3 %all_to_all.21 = f32[16,1,128]{2,1,0:T(1,128)S(1)} all-to-all(f32[16,1,128]{2,1,0:T(1,128)S(1)} %bitcast.12), channel_id=1, replica_groups={{15,14,13,12,11,10,9,8,7,6,5,4,3,2,1,0},{31,30,29,28,27,26,25,24,23,22,..., dimensions={0} | all-to-all | bytes 16384 | tf_op jit(solution)/shard_map/all_to_all | solution.py:121
  22.7 0.5 %reduce_sum.9 = f32[128]{0:T(128)} reduce(f32[16,1,128]{2,1,0:T(1,128)S(1)} %all_to_all.21, f32[]{:T(128)} %constant.23.clone.1), dimensions={0,1}, to_apply=%region_0.1 | reduce | flops 1920 | bytes 8708 | tf_op jit(solution)/shard_map/reduce_sum | solution.py:124

commit v5 on v4

--- a/solution.py
+++ b/solution.py
@@ -9,10 +9,19 @@
 
 LANES = 128
 UNROLLED = 16
+TERMS = 3
 PARAMS = pltpu.CompilerParams(vmem_limit_bytes=8 * 1024 * 1024)
 HBM = pl.BlockSpec(memory_space=pltpu.HBM)
 VMEM = pl.BlockSpec(memory_space=pltpu.VMEM)
 SMEM = pl.BlockSpec(memory_space=pltpu.SMEM)
+
+
+def terms(value):
+    out = []
+    for _ in range(TERMS):
+        out.append(value.astype(jnp.bfloat16).astype(jnp.float32))
+        value = value - out[-1]
+    return out
 
 
 def score_kernel(order, index_ref, spins_hbm, act_hbm, grad_hbm, score_ref, spins_ref, act_ref, grad_ref, sems):
@@ -25,11 +34,12 @@
     for copy in copies:
         copy.wait()
     occupied = spins_ref[...].astype(jnp.float32)
-    weighted = act_ref[...].T * occupied
+    act, grad = terms(act_ref[...]), terms(grad_ref[...])
+    pairs = [(i, j) for i in range(TERMS) for j in range(TERMS - i)]
+    weighted = jnp.concatenate([act[i] for i, _ in pairs], axis=0).T * jnp.concatenate([occupied] * len(pairs), axis=1)
     score = jnp.dot(
-        weighted,
-        grad_ref[...],
-        precision=lax.Precision.HIGHEST,
+        weighted.astype(jnp.bfloat16),
+        jnp.concatenate([grad[j] for _, j in pairs], axis=0).astype(jnp.bfloat16),
         preferred_element_type=jnp.float32,
     )
     slices = len(order) // 2
@@ -85,7 +95,7 @@
     act, grad = activations[0, 0], gradients[0, 0]
     channels, outputs = act.shape[1], grad.shape[1]
     width = n_dev // n_rep
-    order = [place ^ (n_dev - width) for place in range(n_dev)]
+    order = [2 * (i ^ (i >> 1) ^ (n_dev // 4)) + j for j in (1, 0) for i in range(n_dev // 2)]
     members = n_dev * n_rep // 2
     goal = [members - 1 - place for place in range(members)]
     size = channels * outputs // LANES // (n_dev // 2)

time: 23.5 us -> 22.6 us (0.962)
  blocking collectives: 21.3 us -> 20.5 us
    all_to_all x1, blocking collectives: 14 us -> 13 us  [body(): lax.all_to_all(score, 'dev', split_axis=0, concat_axis=0, tiled=True, axi...]
where the time goes in v5:
time: 22.6 us; the launch traced here: 22.4 us
  blocking collectives  20.5 us (91%)
  Pallas kernels  1.34 us (6%)
  other arithmetic  0.54 us (2%)
    all_to_all x1, blocking collectives, body(): lax.all_to_all(score, 'dev', split_axis=0, concat_axis=0, tiled=True, axi...  13 us
    all_to_all x1, blocking collectives, body(): lax.all_to_all(partial, ('dev', 'rep'), split_axis=0, concat_axis=0, tile...  7.45 us
    pallas_call x1, Pallas kernels, body(): pl.pallas_call(functools.partial(score_kernel, order), out_shape=jax.Shap...  1.11 us
    reduce_sum x1, other arithmetic, body(): return jnp.sum(parts, axis=0, keepdims=True)[:, :width]  0.54 us

profile of v5, /device:TPU:0, one launch (start us, length us, event | category | flops | bytes accessed | tf_op | source)
XLA Modules:
  0.0 22.4 jit_solution(12409329193002883913)
XLA Ops:
  0.0 1.1 %score.1 = f32[512,128]{1,0:T(8,128)S(1)} custom-call(s32[1]{0:T(128)} %bitcast.index_ref, s32[1,64]{1,0:T(1,128)} %spins_hbm.1, f32[64,128]{1,0:T(8,128)} %bitcast.14, f32[64,256]{1,0:T(8,128)} %bitcast.13), custom_call_target="tpu_custom_call" | custom-call | tf_op jit(solution)/shard_map/score/pallas_call | solution.py:103
  1.1 13.0 %all_to_all.20 = f32[8,64,128]{2,1,0:T(8,128)S(1)} all-to-all(f32[8,64,128]{2,1,0:T(8,128)S(1)} %bitcast.11), channel_id=1, replica_groups={{20,28,12,4,16,24,8,0},{21,29,13,5,17,25,9,1},{22,30,14,6,18,26,10,2},{..., dimensions={0} | all-to-all | bytes 524288 | tf_op jit(solution)/shard_map/all_to_all | solution.py:117
  14.1 0.2 %gram.1 = f32[16,128]{1,0:T(8,128)S(1)} custom-call(s32[1]{0:T(128)} %bitcast.index_ref, f32[512,128]{1,0:T(8,128)S(1)} %bitcast.10), custom_call_target="tpu_custom_call" | custom-call | tf_op jit(solution)/shard_map/gram/pallas_call | solution.py:118
  14.4 7.5 %all_to_all.21 = f32[16,1,128]{2,1,0:T(1,128)S(1)} all-to-all(f32[16,1,128]{2,1,0:T(1,128)S(1)} %bitcast.12), channel_id=1, replica_groups={{15,14,13,12,11,10,9,8,7,6,5,4,3,2,1,0},{31,30,29,28,27,26,25,24,23,22,..., dimensions={0} | all-to-all | bytes 16384 | tf_op jit(solution)/shard_map/all_to_all | solution.py:131
  21.8 0.5 %reduce_sum.9 = f32[128]{0:T(128)} reduce(f32[16,1,128]{2,1,0:T(1,128)S(1)} %all_to_all.21, f32[]{:T(128)} %constant.23.clone.1), dimensions={0,1}, to_apply=%region_0.1 | reduce | flops 1920 | bytes 8708 | tf_op jit(solution)/shard_map/reduce_sum | solution.py:134

commit v6 on v5

--- a/solution.py
+++ b/solution.py
@@ -25,21 +25,26 @@
 
 
 def score_kernel(order, index_ref, spins_hbm, act_hbm, grad_hbm, score_ref, spins_ref, act_ref, grad_ref, sems):
+    half = grad_hbm.shape[0] // 2
     copies = [
         pltpu.make_async_copy(src, dst, sems.at[i])
-        for i, (src, dst) in enumerate(((grad_hbm, grad_ref), (act_hbm, act_ref), (spins_hbm, spins_ref)))
+        for i, (src, dst) in enumerate((
+            (grad_hbm.at[pl.ds(0, half)], grad_ref.at[pl.ds(0, half)]),
+            (grad_hbm.at[pl.ds(half, half)], grad_ref.at[pl.ds(half, half)]),
+            (act_hbm, act_ref), (spins_hbm, spins_ref)))
     ]
     for copy in copies:
         copy.start()
     for copy in copies:
         copy.wait()
-    occupied = spins_ref[...].astype(jnp.float32)
+    occupied = spins_ref[...].astype(jnp.bfloat16)
     act, grad = terms(act_ref[...]), terms(grad_ref[...])
     pairs = [(i, j) for i in range(TERMS) for j in range(TERMS - i)]
-    weighted = jnp.concatenate([act[i] for i, _ in pairs], axis=0).T * jnp.concatenate([occupied] * len(pairs), axis=1)
+    weighted = jnp.concatenate([act[i].astype(jnp.bfloat16) for i, _ in pairs], axis=0).T
+    weighted = weighted * jnp.concatenate([occupied] * len(pairs), axis=1)
     score = jnp.dot(
-        weighted.astype(jnp.bfloat16),
-        jnp.concatenate([grad[j] for _, j in pairs], axis=0).astype(jnp.bfloat16),
+        weighted,
+        jnp.concatenate([grad[j].astype(jnp.bfloat16) for _, j in pairs], axis=0),
         preferred_element_type=jnp.float32,
     )
     slices = len(order) // 2
@@ -109,7 +114,7 @@
             pltpu.VMEM(spins.shape, spins.dtype),
             pltpu.VMEM(act.shape, act.dtype),
             pltpu.VMEM(grad.shape, grad.dtype),
-            pltpu.SemaphoreType.DMA((3,)),
+            pltpu.SemaphoreType.DMA((4,)),
         ],
         compiler_params=PARAMS,
         name="score",

time: 22.6 us -> 22.6 us (level)
  no operation moved by 1% of the time
where the time goes in v6:
time: 22.6 us; the launch traced here: 22.3 us
  blocking collectives  20.5 us (91%)
  Pallas kernels  1.28 us (6%)
  other arithmetic  0.54 us (2%)
    all_to_all x1, blocking collectives, body(): lax.all_to_all(score, 'dev', split_axis=0, concat_axis=0, tiled=True, axi...  13 us
    all_to_all x1, blocking collectives, body(): lax.all_to_all(partial, ('dev', 'rep'), split_axis=0, concat_axis=0, tile...  7.45 us
    pallas_call x1, Pallas kernels, body(): pl.pallas_call(functools.partial(score_kernel, order), out_shape=jax.Shap...  1.06 us
    reduce_sum x1, other arithmetic, body(): return jnp.sum(parts, axis=0, keepdims=True)[:, :width]  0.54 us

profile of v6, /device:TPU:0, one launch (start us, length us, event | category | flops | bytes accessed | tf_op | source)
XLA Modules:
  0.0 22.3 jit_solution(14820507245113577052)
XLA Ops:
  0.0 1.1 %score.1 = f32[512,128]{1,0:T(8,128)S(1)} custom-call(s32[1]{0:T(128)} %bitcast.index_ref, s32[1,64]{1,0:T(1,128)} %spins_hbm.1, f32[64,128]{1,0:T(8,128)} %bitcast.14, f32[64,256]{1,0:T(8,128)} %bitcast.13), custom_call_target="tpu_custom_call" | custom-call | tf_op jit(solution)/shard_map/score/pallas_call | solution.py:108
  1.1 13.0 %all_to_all.20 = f32[8,64,128]{2,1,0:T(8,128)S(1)} all-to-all(f32[8,64,128]{2,1,0:T(8,128)S(1)} %bitcast.11), channel_id=1, replica_groups={{20,28,12,4,16,24,8,0},{21,29,13,5,17,25,9,1},{22,30,14,6,18,26,10,2},{..., dimensions={0} | all-to-all | bytes 524288 | tf_op jit(solution)/shard_map/all_to_all | solution.py:122
  14.1 0.2 %gram.1 = f32[16,128]{1,0:T(8,128)S(1)} custom-call(s32[1]{0:T(128)} %bitcast.index_ref, f32[512,128]{1,0:T(8,128)S(1)} %bitcast.10), custom_call_target="tpu_custom_call" | custom-call | tf_op jit(solution)/shard_map/gram/pallas_call | solution.py:123
  14.3 7.5 %all_to_all.21 = f32[16,1,128]{2,1,0:T(1,128)S(1)} all-to-all(f32[16,1,128]{2,1,0:T(1,128)S(1)} %bitcast.12), channel_id=1, replica_groups={{15,14,13,12,11,10,9,8,7,6,5,4,3,2,1,0},{31,30,29,28,27,26,25,24,23,22,..., dimensions={0} | all-to-all | bytes 16384 | tf_op jit(solution)/shard_map/all_to_all | solution.py:136
  21.8 0.5 %reduce_sum.9 = f32[128]{0:T(128)} reduce(f32[16,1,128]{2,1,0:T(1,128)S(1)} %all_to_all.21, f32[]{:T(128)} %constant.23.clone.1), dimensions={0,1}, to_apply=%region_0.1 | reduce | flops 1920 | bytes 8708 | tf_op jit(solution)/shard_map/reduce_sum | solution.py:139

commit v7 on v5

--- a/solution.py
+++ b/solution.py
@@ -24,7 +24,7 @@
     return out
 
 
-def score_kernel(order, index_ref, spins_hbm, act_hbm, grad_hbm, score_ref, spins_ref, act_ref, grad_ref, sems):
+def score_kernel(orders, index_ref, spins_hbm, act_hbm, grad_hbm, score_ref, spins_ref, act_ref, grad_ref, sems):
     copies = [
         pltpu.make_async_copy(src, dst, sems.at[i])
         for i, (src, dst) in enumerate(((grad_hbm, grad_ref), (act_hbm, act_ref), (spins_hbm, spins_ref)))
@@ -42,15 +42,16 @@
         jnp.concatenate([grad[j] for _, j in pairs], axis=0).astype(jnp.bfloat16),
         preferred_element_type=jnp.float32,
     )
-    slices = len(order) // 2
+    slices = len(orders[0]) // 2
     rows = score.shape[0] // slices
     parts = score.shape[1] // LANES
-    for place, owner in enumerate(order):
-        piece = owner % slices
+    odd = index_ref[0] % 2 != 0
+    for place, owners in enumerate(zip(*orders)):
+        pieces = [owner % slices for owner in owners]
+        blocks = [score[piece * rows : (piece + 1) * rows, :] for piece in pieces]
+        block = blocks[0] if pieces[0] == pieces[1] else jnp.where(odd, blocks[1], blocks[0])
         for part in range(parts):
-            score_ref[pl.ds((place * parts + part) * rows, rows), :] = score[
-                piece * rows : (piece + 1) * rows, part * LANES : (part + 1) * LANES
-            ]
+            score_ref[pl.ds((place * parts + part) * rows, rows), :] = block[:, part * LANES : (part + 1) * LANES]
 
 
 def each(count, step):
@@ -61,16 +62,17 @@
         pl.loop(0, count)(step)
 
 
-def gram_kernel(order, members, shares, index_ref, moved_ref, gram_ref, centered_ref, lanes_ref):
-    samples = len(order)
+def gram_kernel(orders, members, shares, index_ref, moved_ref, gram_ref, centered_ref, lanes_ref):
+    samples = len(orders[0])
+    odd = index_ref[0] % 2 != 0
     width = samples // shares
     rows = moved_ref.shape[0] // samples
     scores = [moved_ref[pl.ds(place * rows, rows), :] for place in range(samples)]
     mean = functools.reduce(jnp.add, scores) * (1.0 / samples)
-    for place, owner in enumerate(order):
-        centered_ref[owner] = scores[place] - mean
+    for place, (even_owner, odd_owner) in enumerate(zip(*orders)):
+        centered_ref[jnp.where(odd, odd_owner, even_owner)] = scores[place] - mean
     mine = members // shares
-    first = index_ref[0] * mine
+    first = index_ref[0] // 2 * mine
 
     def row_step(row):
         own = centered_ref[first + row]
@@ -95,13 +97,20 @@
     act, grad = activations[0, 0], gradients[0, 0]
     channels, outputs = act.shape[1], grad.shape[1]
     width = n_dev // n_rep
-    order = [2 * (i ^ (i >> 1) ^ (n_dev // 4)) + j for j in (1, 0) for i in range(n_dev // 2)]
+    layers = n_dev // 2
+    orders = [
+        [2 * layer + j for j in (1, 0) for layer in along]
+        for along in (
+            [i ^ (i >> 1) ^ (layers // 2) for i in range(layers)],
+            [(layers // 2 - i) % layers for i in range(layers)],
+        )
+    ]
     members = n_dev * n_rep // 2
     goal = [members - 1 - place for place in range(members)]
     size = channels * outputs // LANES // (n_dev // 2)
-    index = (lax.axis_index("dev") // (n_dev // 2)).astype(jnp.int32).reshape(1)
+    index = (lax.axis_index("dev") // (n_dev // 2) * 2 + lax.axis_index("rep") % 2).astype(jnp.int32).reshape(1)
     score = pl.pallas_call(
-        functools.partial(score_kernel, order),
+        functools.partial(score_kernel, orders),
         out_shape=jax.ShapeDtypeStruct((n_dev * size, LANES), jnp.float32),
         in_specs=[SMEM, HBM, HBM, HBM],
         out_specs=VMEM,
@@ -114,9 +123,12 @@
         compiler_params=PARAMS,
         name="score",
     )(index, *(pltpu.with_memory_space_constraint(x, pltpu.HBM) for x in (spins, act, grad)))
-    moved = lax.all_to_all(score, "dev", split_axis=0, concat_axis=0, tiled=True, axis_index_groups=[order])
+    columns = [[d * n_rep + r for d in orders[r % 2]] for r in range(n_rep)]
+    moved = lax.all_to_all(
+        score, ("dev", "rep"), split_axis=0, concat_axis=0, tiled=True, axis_index_groups=columns
+    )
     partial = pl.pallas_call(
-        functools.partial(gram_kernel, order, members, n_rep),
+        functools.partial(gram_kernel, orders, members, n_rep),
         out_shape=jax.ShapeDtypeStruct((members, LANES), jnp.float32),
         in_specs=[SMEM, VMEM],
         out_specs=VMEM,

time: 22.6 us -> 22.4 us (level)
    all_to_all x1, blocking collectives: 7.45 us -> 7.15 us  [body(): lax.all_to_all(partial, ('dev', 'rep'), split_axis=0, concat_axis=0, tile...]
where the time goes in v7:
time: 22.4 us; the launch traced here: 22.2 us
  blocking collectives  20.3 us (91%)
  Pallas kernels  1.34 us (6%)
  other arithmetic  0.54 us (2%)
    all_to_all x1, blocking collectives, body(): lax.all_to_all(score, ('dev', 'rep'), split_axis=0, concat_axis=0, tiled=...  13.2 us
    all_to_all x1, blocking collectives, body(): lax.all_to_all(partial, ('dev', 'rep'), split_axis=0, concat_axis=0, tile...  7.15 us
    pallas_call x1, Pallas kernels, body(): pl.pallas_call(functools.partial(score_kernel, orders), out_shape=jax.Sha...  1.11 us
    reduce_sum x1, other arithmetic, body(): return jnp.sum(parts, axis=0, keepdims=True)[:, :width]  0.54 us

profile of v7, /device:TPU:0, one launch (start us, length us, event | category | flops | bytes accessed | tf_op | source)
XLA Modules:
  0.0 22.2 jit_solution(9429663882554952300)
XLA Ops:
  0.0 1.1 %score.1 = f32[512,128]{1,0:T(8,128)S(1)} custom-call(s32[1]{0:T(128)} %bitcast.index_ref, s32[1,64]{1,0:T(1,128)} %spins_hbm.1, f32[64,128]{1,0:T(8,128)} %bitcast.14, f32[64,256]{1,0:T(8,128)} %bitcast.13), custom_call_target="tpu_custom_call" | custom-call | tf_op jit(solution)/shard_map/score/pallas_call | solution.py:112
  1.1 13.2 %all_to_all.20 = f32[8,64,128]{2,1,0:T(8,128)S(1)} all-to-all(f32[8,64,128]{2,1,0:T(8,128)S(1)} %bitcast.11), channel_id=1, replica_groups={{20,28,12,4,16,24,8,0},{21,13,5,29,17,9,1,25},{22,30,14,6,18,26,10,2},{..., dimensions={0} | all-to-all | bytes 524288 | tf_op jit(solution)/shard_map/all_to_all | solution.py:127
  14.3 0.2 gram.1
  14.5 7.2 %all_to_all.21 = f32[16,1,128]{2,1,0:T(1,128)S(1)} all-to-all(f32[16,1,128]{2,1,0:T(1,128)S(1)} %bitcast.12), channel_id=1, replica_groups={{15,14,13,12,11,10,9,8,7,6,5,4,3,2,1,0},{31,30,29,28,27,26,25,24,23,22,..., dimensions={0} | all-to-all | bytes 16384 | tf_op jit(solution)/shard_map/all_to_all | solution.py:143
  21.7 0.5 %reduce_sum.9 = f32[128]{0:T(128)} reduce(f32[16,1,128]{2,1,0:T(1,128)S(1)} %all_to_all.21, f32[]{:T(128)} %constant.36.clone.1), dimensions={0,1}, to_apply=%region_0.1 | reduce | flops 1920 | bytes 8708 | tf_op jit(solution)/shard_map/reduce_sum | solution.py:146

commit v8 on v7

--- a/solution.py
+++ b/solution.py
@@ -25,21 +25,26 @@
 
 
 def score_kernel(orders, index_ref, spins_hbm, act_hbm, grad_hbm, score_ref, spins_ref, act_ref, grad_ref, sems):
+    half = grad_hbm.shape[0] // 2
     copies = [
         pltpu.make_async_copy(src, dst, sems.at[i])
-        for i, (src, dst) in enumerate(((grad_hbm, grad_ref), (act_hbm, act_ref), (spins_hbm, spins_ref)))
+        for i, (src, dst) in enumerate((
+            (grad_hbm.at[pl.ds(0, half)], grad_ref.at[pl.ds(0, half)]),
+            (grad_hbm.at[pl.ds(half, half)], grad_ref.at[pl.ds(half, half)]),
+            (act_hbm, act_ref), (spins_hbm, spins_ref)))
     ]
     for copy in copies:
         copy.start()
     for copy in copies:
         copy.wait()
-    occupied = spins_ref[...].astype(jnp.float32)
+    occupied = spins_ref[...].astype(jnp.bfloat16)
     act, grad = terms(act_ref[...]), terms(grad_ref[...])
     pairs = [(i, j) for i in range(TERMS) for j in range(TERMS - i)]
-    weighted = jnp.concatenate([act[i] for i, _ in pairs], axis=0).T * jnp.concatenate([occupied] * len(pairs), axis=1)
+    weighted = jnp.concatenate([act[i].astype(jnp.bfloat16) for i, _ in pairs], axis=0).T
+    weighted = weighted * jnp.concatenate([occupied] * len(pairs), axis=1)
     score = jnp.dot(
-        weighted.astype(jnp.bfloat16),
-        jnp.concatenate([grad[j] for _, j in pairs], axis=0).astype(jnp.bfloat16),
+        weighted,
+        jnp.concatenate([grad[j].astype(jnp.bfloat16) for _, j in pairs], axis=0),
         preferred_element_type=jnp.float32,
     )
     slices = len(orders[0]) // 2
@@ -118,7 +123,7 @@
             pltpu.VMEM(spins.shape, spins.dtype),
             pltpu.VMEM(act.shape, act.dtype),
             pltpu.VMEM(grad.shape, grad.dtype),
-            pltpu.SemaphoreType.DMA((3,)),
+            pltpu.SemaphoreType.DMA((4,)),
         ],
         compiler_params=PARAMS,
         name="score",

time: 22.4 us -> 22.4 us (level)
  no operation moved by 1% of the time
where the time goes in v8:
time: 22.4 us; the launch traced here: 22.1 us
  blocking collectives  20.3 us (91%)
  Pallas kernels  1.28 us (6%)
  other arithmetic  0.54 us (2%)
    all_to_all x1, blocking collectives, body(): lax.all_to_all(score, ('dev', 'rep'), split_axis=0, concat_axis=0, tiled=...  13.2 us
    all_to_all x1, blocking collectives, body(): lax.all_to_all(partial, ('dev', 'rep'), split_axis=0, concat_axis=0, tile...  7.15 us
    pallas_call x1, Pallas kernels, body(): pl.pallas_call(functools.partial(score_kernel, orders), out_shape=jax.Sha...  1.06 us
    reduce_sum x1, other arithmetic, body(): return jnp.sum(parts, axis=0, keepdims=True)[:, :width]  0.54 us

profile of v8, /device:TPU:0, one launch (start us, length us, event | category | flops | bytes accessed | tf_op | source)
XLA Modules:
  0.0 22.1 jit_solution(1925151653053886755)
XLA Ops:
  0.0 1.1 %score.1 = f32[512,128]{1,0:T(8,128)S(1)} custom-call(s32[1]{0:T(128)} %bitcast.index_ref, s32[1,64]{1,0:T(1,128)} %spins_hbm.1, f32[64,128]{1,0:T(8,128)} %bitcast.14, f32[64,256]{1,0:T(8,128)} %bitcast.13), custom_call_target="tpu_custom_call" | custom-call | tf_op jit(solution)/shard_map/score/pallas_call | solution.py:117
  1.1 13.2 %all_to_all.20 = f32[8,64,128]{2,1,0:T(8,128)S(1)} all-to-all(f32[8,64,128]{2,1,0:T(8,128)S(1)} %bitcast.11), channel_id=1, replica_groups={{20,28,12,4,16,24,8,0},{21,13,5,29,17,9,1,25},{22,30,14,6,18,26,10,2},{..., dimensions={0} | all-to-all | bytes 524288 | tf_op jit(solution)/shard_map/all_to_all | solution.py:132
  14.2 0.2 %gram.1 = f32[16,128]{1,0:T(8,128)S(1)} custom-call(s32[1]{0:T(128)} %bitcast.index_ref, f32[512,128]{1,0:T(8,128)S(1)} %bitcast.10), custom_call_target="tpu_custom_call" | custom-call | tf_op jit(solution)/shard_map/gram/pallas_call | solution.py:135
  14.5 7.2 %all_to_all.21 = f32[16,1,128]{2,1,0:T(1,128)S(1)} all-to-all(f32[16,1,128]{2,1,0:T(1,128)S(1)} %bitcast.12), channel_id=1, replica_groups={{15,14,13,12,11,10,9,8,7,6,5,4,3,2,1,0},{31,30,29,28,27,26,25,24,23,22,..., dimensions={0} | all-to-all | bytes 16384 | tf_op jit(solution)/shard_map/all_to_all | solution.py:148
  21.6 0.5 %reduce_sum.9 = f32[128]{0:T(128)} reduce(f32[16,1,128]{2,1,0:T(1,128)S(1)} %all_to_all.21, f32[]{:T(128)} %constant.36.clone.1), dimensions={0,1}, to_apply=%region_0.1 | reduce | flops 1920 | bytes 8708 | tf_op jit(solution)/shard_map/reduce_sum | solution.py:151

commit v9 on v8

--- a/solution.py
+++ b/solution.py
@@ -35,13 +35,16 @@
     ]
     for copy in copies:
         copy.start()
-    for copy in copies:
+    for copy in copies[2:]:
         copy.wait()
     occupied = spins_ref[...].astype(jnp.bfloat16)
-    act, grad = terms(act_ref[...]), terms(grad_ref[...])
+    act = terms(act_ref[...])
     pairs = [(i, j) for i in range(TERMS) for j in range(TERMS - i)]
     weighted = jnp.concatenate([act[i].astype(jnp.bfloat16) for i, _ in pairs], axis=0).T
     weighted = weighted * jnp.concatenate([occupied] * len(pairs), axis=1)
+    for copy in copies[:2]:
+        copy.wait()
+    grad = terms(grad_ref[...])
     score = jnp.dot(
         weighted,
         jnp.concatenate([grad[j].astype(jnp.bfloat16) for _, j in pairs], axis=0),

time: 22.4 us -> 22.4 us (level)
  no operation moved by 1% of the time
where the time goes in v9:
time: 22.4 us; the launch traced here: 22.2 us
  blocking collectives  20.3 us (91%)
  Pallas kernels  1.33 us (6%)
  other arithmetic  0.54 us (2%)
    all_to_all x1, blocking collectives, body(): lax.all_to_all(score, ('dev', 'rep'), split_axis=0, concat_axis=0, tiled=...  13.2 us
    all_to_all x1, blocking collectives, body(): lax.all_to_all(partial, ('dev', 'rep'), split_axis=0, concat_axis=0, tile...  7.15 us
    pallas_call x1, Pallas kernels, body(): pl.pallas_call(functools.partial(score_kernel, orders), out_shape=jax.Sha...  1.1 us
    reduce_sum x1, other arithmetic, body(): return jnp.sum(parts, axis=0, keepdims=True)[:, :width]  0.54 us

profile of v9, /device:TPU:0, one launch (start us, length us, event | category | flops | bytes accessed | tf_op | source)
XLA Modules:
  0.0 22.2 jit_solution(10529258017939184515)
XLA Ops:
  0.0 1.1 %score.1 = f32[512,128]{1,0:T(8,128)S(1)} custom-call(s32[1]{0:T(128)} %bitcast.index_ref, s32[1,64]{1,0:T(1,128)} %spins_hbm.1, f32[64,128]{1,0:T(8,128)} %bitcast.14, f32[64,256]{1,0:T(8,128)} %bitcast.13), custom_call_target="tpu_custom_call" | custom-call | tf_op jit(solution)/shard_map/score/pallas_call | solution.py:120
  1.1 13.2 %all_to_all.20 = f32[8,64,128]{2,1,0:T(8,128)S(1)} all-to-all(f32[8,64,128]{2,1,0:T(8,128)S(1)} %bitcast.11), channel_id=1, replica_groups={{20,28,12,4,16,24,8,0},{21,13,5,29,17,9,1,25},{22,30,14,6,18,26,10,2},{..., dimensions={0} | all-to-all | bytes 524288 | tf_op jit(solution)/shard_map/all_to_all | solution.py:135
  14.3 0.2 gram.1
  14.5 7.2 %all_to_all.21 = f32[16,1,128]{2,1,0:T(1,128)S(1)} all-to-all(f32[16,1,128]{2,1,0:T(1,128)S(1)} %bitcast.12), channel_id=1, replica_groups={{15,14,13,12,11,10,9,8,7,6,5,4,3,2,1,0},{31,30,29,28,27,26,25,24,23,22,..., dimensions={0} | all-to-all | bytes 16384 | tf_op jit(solution)/shard_map/all_to_all | solution.py:151
  21.7 0.5 %reduce_sum.9 = f32[128]{0:T(128)} reduce(f32[16,1,128]{2,1,0:T(1,128)S(1)} %all_to_all.21, f32[]{:T(128)} %constant.36.clone.1), dimensions={0,1}, to_apply=%region_0.1 | reduce | flops 1920 | bytes 8708 | tf_op jit(solution)/shard_map/reduce_sum | solution.py:154

commit v10 on v9

--- a/solution.py
+++ b/solution.py
@@ -33,7 +33,7 @@
             (grad_hbm.at[pl.ds(half, half)], grad_ref.at[pl.ds(half, half)]),
             (act_hbm, act_ref), (spins_hbm, spins_ref)))
     ]
-    for copy in copies:
+    for copy in copies[2:] + copies[:2]:
         copy.start()
     for copy in copies[2:]:
         copy.wait()

time: 22.4 us -> 22.4 us (level)
  no operation moved by 1% of the time
where the time goes in v10:
time: 22.4 us; the launch traced here: 22.2 us
  blocking collectives  20.3 us (91%)
  Pallas kernels  1.3 us (6%)
  other arithmetic  0.54 us (2%)
    all_to_all x1, blocking collectives, body(): lax.all_to_all(score, ('dev', 'rep'), split_axis=0, concat_axis=0, tiled=...  13.2 us
    all_to_all x1, blocking collectives, body(): lax.all_to_all(partial, ('dev', 'rep'), split_axis=0, concat_axis=0, tile...  7.15 us
    pallas_call x1, Pallas kernels, body(): pl.pallas_call(functools.partial(score_kernel, orders), out_shape=jax.Sha...  1.08 us
    reduce_sum x1, other arithmetic, body(): return jnp.sum(parts, axis=0, keepdims=True)[:, :width]  0.54 us

profile of v10, /device:TPU:0, one launch (start us, length us, event | category | flops | bytes accessed | tf_op | source)
XLA Modules:
  0.0 22.2 jit_solution(15916530688021259539)
XLA Ops:
  0.0 1.1 %score.1 = f32[512,128]{1,0:T(8,128)S(1)} custom-call(s32[1]{0:T(128)} %bitcast.index_ref, s32[1,64]{1,0:T(1,128)} %spins_hbm.1, f32[64,128]{1,0:T(8,128)} %bitcast.14, f32[64,256]{1,0:T(8,128)} %bitcast.13), custom_call_target="tpu_custom_call" | custom-call | tf_op jit(solution)/shard_map/score/pallas_call | solution.py:120
  1.1 13.2 %all_to_all.20 = f32[8,64,128]{2,1,0:T(8,128)S(1)} all-to-all(f32[8,64,128]{2,1,0:T(8,128)S(1)} %bitcast.11), channel_id=1, replica_groups={{20,28,12,4,16,24,8,0},{21,13,5,29,17,9,1,25},{22,30,14,6,18,26,10,2},{..., dimensions={0} | all-to-all | bytes 524288 | tf_op jit(solution)/shard_map/all_to_all | solution.py:135
  14.2 0.2 gram.1
  14.5 7.2 %all_to_all.21 = f32[16,1,128]{2,1,0:T(1,128)S(1)} all-to-all(f32[16,1,128]{2,1,0:T(1,128)S(1)} %bitcast.12), channel_id=1, replica_groups={{15,14,13,12,11,10,9,8,7,6,5,4,3,2,1,0},{31,30,29,28,27,26,25,24,23,22,..., dimensions={0} | all-to-all | bytes 16384 | tf_op jit(solution)/shard_map/all_to_all | solution.py:151
  21.6 0.5 %reduce_sum.9 = f32[128]{0:T(128)} reduce(f32[16,1,128]{2,1,0:T(1,128)S(1)} %all_to_all.21, f32[]{:T(128)} %constant.36.clone.1), dimensions={0,1}, to_apply=%region_0.1 | reduce | flops 1920 | bytes 8708 | tf_op jit(solution)/shard_map/reduce_sum | solution.py:154
